TPU v7x, 32 devices: a whole 2x2x4 slice. The times are simulated.
32 devices in a mesh: groups: 2 (over y), scanx: 4 (over z), scany: 2 (over x), pos: 2 (over core).
Axes of the slice: x: 2, y: 2, z: 4, core: 2. Of those that a mesh axis runs over, the one named last changes fastest.
Arguments:
- specimen: float32 [2, 2048, 512], P(None, ('groups', 'scanx'), 'scany'), parts along dimension 1, may hold values from -5 to 5
- probe_wave: float32 [2, 512, 256], P(None, 'groups'), parts along dimension 1, may hold values from -6 to 6
- amplitudes: bfloat16 [64, 256, 256], P(('groups', 'scanx', 'scany', 'pos')), parts along dimension 0, may hold values from 0 to 2
- offsets: int32 [64, 2], P(('groups', 'scanx', 'scany', 'pos')), parts along dimension 0, may hold values from 0 to 255
Outputs:
- new_specimen: float32 [2, 2048, 512], P(None, ('groups', 'scanx'), 'scany'), parts along dimension 1
- new_probe: float32 [2, 512, 256], P(None, 'groups'), parts along dimension 1
There are 2 independent parts, one for each index of `groups`. A program takes and returns all parts, laid end to end along the dimension named above; each array names one. Nothing has to cross between parts.
Inputs may be any that keep to these rules, and one draw needn't show every extreme that they name: offsets are pixels from the top-left corner of the position's tile.
All inputs are finite; a program needn't handle non-finite values.
Results may differ from a plain program's by a relative error of at most 0.002.
The roundings to bfloat16 on the way count: a program that leaves them out, or rounds other values in their place, can miss the bound.
Values sent between devices are 32-bit elements; how exact they have to be, the bound alone decides.
A program may use at most 64 MiB of HBM per device.

v0:
```python
import math
import jax
import jax.numpy as jnp
from jax import lax
from jax.sharding import PartitionSpec as P


def padded_2(block, sides, width):
    for axis, dim in sides:
        count = lax.axis_size(axis)
        forward = [(i, i + 1) for i in range(count - 1)]
        backward = [(target, source) for source, target in forward]
        low = lax.ppermute(
            lax.slice_in_dim(block, block.shape[dim] - width, None, axis=dim), axis, forward
        )
        high = lax.ppermute(lax.slice_in_dim(block, 0, width, axis=dim), axis, backward)
        block = jnp.concatenate([low, block, high], axis=dim)
    return block


def dft_tables(length):
    positions_index = jnp.arange(length, dtype=jnp.int32)
    phase_index = positions_index[:, None] * positions_index[None, :] % length
    angle_rad = phase_index.astype(jnp.float32) * (2.0 * math.pi / length)
    scale_factor = 1.0 / math.sqrt(length)
    cosine = (jnp.cos(angle_rad) * scale_factor).astype(jnp.bfloat16)
    sine_part = (jnp.sin(angle_rad) * scale_factor).astype(jnp.bfloat16)
    forward_left = jnp.stack(
        [jnp.stack([cosine, sine_part], 1), jnp.stack([-sine_part, cosine], 1)], 0
    )
    forward_right = jnp.stack(
        [jnp.stack([cosine, -sine_part], 1), jnp.stack([sine_part, cosine], 1)], 0
    )
    inverse_left = jnp.stack(
        [jnp.stack([cosine, -sine_part], 1), jnp.stack([sine_part, cosine], 1)], 0
    )
    inverse_right = jnp.stack(
        [jnp.stack([cosine, sine_part], 1), jnp.stack([-sine_part, cosine], 1)], 0
    )
    return (forward_left, forward_right, inverse_left, inverse_right)


def project_exit(patch_wave, probe_real, probe_imag, amplitude, tables):
    forward_left, forward_right, inverse_left, inverse_right = tables
    patch_real = patch_wave[0]
    patch_imag = patch_wave[1]
    exit_real = probe_real * patch_real - probe_imag * patch_imag
    exit_imag = probe_real * patch_imag + probe_imag * patch_real
    exit_wave = jnp.stack([exit_real, exit_imag]).astype(jnp.bfloat16)
    half_done = jnp.einsum(
        "akbr,brv->akv", forward_left, exit_wave, preferred_element_type=jnp.float32
    ).astype(jnp.bfloat16)
    far_field = jnp.einsum(
        "bkv,bval->akl", half_done, forward_right, preferred_element_type=jnp.float32
    )
    magnitude = jnp.sqrt(far_field[0] * far_field[0] + far_field[1] * far_field[1])
    scale_ratio = amplitude.astype(jnp.float32) / jnp.maximum(magnitude, 0.2)
    projected = (far_field * scale_ratio[None]).astype(jnp.bfloat16)
    back_half = jnp.einsum(
        "akbr,brv->akv", inverse_left, projected, preferred_element_type=jnp.float32
    ).astype(jnp.bfloat16)
    back_wave = jnp.einsum(
        "bkv,bval->akl", back_half, inverse_right, preferred_element_type=jnp.float32
    )
    return (back_wave[0] - exit_real, back_wave[1] - exit_imag, patch_real, patch_imag)


def fold_margin(field_in, axis_dim, margin, tile_len):
    extent = field_in.shape[axis_dim]
    inner_part = lax.slice_in_dim(field_in, 2 * margin, 2 * margin + tile_len, axis=axis_dim)
    lower_rim = lax.slice_in_dim(field_in, 0, margin, axis=axis_dim)
    upper_rim = lax.slice_in_dim(field_in, extent - margin, extent, axis=axis_dim)
    lower_widths = [(0, 0)] * field_in.ndim
    upper_widths = [(0, 0)] * field_in.ndim
    lower_widths[axis_dim] = (0, tile_len - margin)
    upper_widths[axis_dim] = (tile_len - margin, 0)
    return inner_part + jnp.pad(lower_rim, lower_widths) + jnp.pad(upper_rim, upper_widths)


def shards(specimen, probe_wave, amplitudes, offsets):
    pattern = probe_wave.shape[1]
    margin = pattern // 2
    tile_len = specimen.shape[1]
    tables = dft_tables(pattern)
    padded = padded_2(specimen, (("scanx", 1), ("scany", 2)), margin)
    probe_real = probe_wave[0]
    probe_imag = probe_wave[1]
    probe_power = probe_real * probe_real + probe_imag * probe_imag
    zero_index = jnp.zeros((), jnp.int32)

    def visit_position(carried, inputs):
        object_grad, probe_grad = carried
        amplitude, offset = inputs
        row_start = offset[0]
        col_start = offset[1]
        patch_wave = lax.dynamic_slice(
            padded, (zero_index, row_start, col_start), (2, pattern, pattern)
        )
        diff_real, diff_imag, patch_real, patch_imag = project_exit(
            patch_wave, probe_real, probe_imag, amplitude, tables
        )
        object_term = jnp.stack(
            [
                probe_real * diff_real + probe_imag * diff_imag,
                probe_real * diff_imag - probe_imag * diff_real,
                probe_power,
            ]
        )
        current = lax.dynamic_slice(
            object_grad, (zero_index, row_start, col_start), (3, pattern, pattern)
        )
        object_grad = lax.dynamic_update_slice(
            object_grad, current + object_term, (zero_index, row_start, col_start)
        )
        probe_term = jnp.stack(
            [
                patch_real * diff_real + patch_imag * diff_imag,
                patch_real * diff_imag - patch_imag * diff_real,
            ]
        )
        return ((object_grad, probe_grad + probe_term), None)

    start_grad = jnp.zeros((3, tile_len + pattern, tile_len + pattern), jnp.float32)
    start_probe = jnp.zeros((2, pattern, pattern), jnp.float32)
    (object_grad, probe_grad), unused = lax.scan(
        visit_position, (start_grad, start_probe), (amplitudes, offsets)
    )
    row_halo = padded_2(object_grad, (("scanx", 1),), margin)
    row_folded = fold_margin(row_halo, 1, margin, tile_len)
    col_halo = padded_2(row_folded, (("scany", 2),), margin)
    core_sum = fold_margin(col_halo, 2, margin, tile_len)
    core_sum = lax.psum(core_sum, "pos")
    new_specimen = specimen + core_sum[0:2] / (core_sum[2:3] + 1.0)
    devices_count = lax.axis_size("scanx") * lax.axis_size("scany") * lax.axis_size("pos")
    step_size = 1.0 / math.sqrt(offsets.shape[0] * devices_count)
    total_grad = lax.psum(probe_grad, ("scanx", "scany", "pos"))
    new_probe = probe_wave + total_grad * step_size
    return (new_specimen, new_probe)


def solution(mesh):
    placed = (
        P(None, ("groups", "scanx"), "scany"),
        P(None, "groups", None),
        P(("groups", "scanx", "scany", "pos"), None, None),
        P(("groups", "scanx", "scany", "pos"), None),
    )
    return jax.shard_map(
        shards,
        mesh=mesh,
        in_specs=placed,
        out_specs=(P(None, ("groups", "scanx"), "scany"), P(None, "groups", None)),
        check_vma=False,
    )
```

profile of v0, /device:TPU:0, one launch (start us, length us, event | category | flops | bytes accessed | tf_op | source)
XLA Modules:
  0.0 249.2 jit_solution(168859406196740415)
XLA Ops:
  7.2 1.1 fusion.50
  8.3 1.3 collective-permute-start.1
  9.6 5.6 %collective-permute-start = (f32[2,128,256]{2,1,0:T(8,128)S(1)}, f32[2,128,256]{2,1,0:T(8,128)S(1)}, u32[]{:S(2)}, u32[]{:S(2)}) collective-permute-start(f32[2,128,256]{2,1,0:T(8,128)S(1)} %get-tuple-element.187), channel_id=1, source_target_pairs={{0,4},{4,8},{8,12},{1,5},{5,9},{9,13},{2,6},{6,10},{10,14},{3,7},{... | collective-permute-start | bytes 786440 | tf_op jit(solution)/shard_map/ppermute | solution.py:13
  15.2 1.0 fusion.41
  16.2 1.1 multiply_convert_fusion.1
  18.3 2.5 collective-permute-done
  20.9 0.9 fusion.49
  21.8 4.4 %collective-permute-start.2 = (f32[2,512,128]{2,1,0:T(8,128)}, f32[2,512,128]{2,1,0:T(8,128)}, u32[]{:S(2)}, u32[]{:S(2)}) collective-permute-start(f32[2,512,128]{2,1,0:T(8,128)} %get-tuple-element.182), channel_id=1, source_target_pairs={{0,2},{1,3},{4,6},{5,7},{8,10},{9,11},{12,14},{13,15},{16,18},{17,... | collective-permute-start | bytes 1572872 | tf_op jit(solution)/shard_map/ppermute | solution.py:13
  26.1 1.3 collective-permute-start.3
  29.8 5.9 %collective-permute-done.2 = f32[2,512,128]{2,1,0:T(8,128)} collective-permute-done((f32[2,512,128]{2,1,0:T(8,128)}, f32[2,512,128]{2,1,0:T(8,128)}, u32[]{:S(2)}, u32[]{:S(2)}) %collective-permute-start.2) | collective-permute-done | bytes 524320 | tf_op jit(solution)/shard_map/ppermute | solution.py:13
  35.7 4.7 %collective-permute-done.3 = f32[2,512,128]{2,1,0:T(8,128)} collective-permute-done((f32[2,512,128]{2,1,0:T(8,128)S(1)}, f32[2,512,128]{2,1,0:T(8,128)}, u32[]{:S(2)}, u32[]{:S(2)}) %collective-permute-start.3) | collective-permute-done | bytes 524320 | tf_op jit(solution)/shard_map/ppermute | solution.py:16
  40.4 1.4 pad_maximum_fusion
  41.8 2.0 broadcast_in_dim.10
  43.8 53.8 %while.14 = (s32[]{:T(128)}, f32[3,512,512]{2,1,0:T(8,128)}, f32[2,256,256]{2,1,0:T(8,128)}, s32[2,2]{1,0:T(2,128)S(1)}, f32[256,256]{1,0:T(8,128)}, /*index=5*/...) while((s32[]{:T(128)}, f32[3,512,512]{2,1,0:T(8,128)}, ...), condition=%wide.region_1.2_spmd.clone, body=%wide.region_0.1_spmd.clone.sunk | while | flops 540737536 | bytes 17170760 | solution.py:125
  48.2 2.0 fusion.72
  50.1 1.9 convolution_bitcast_fusion.6
  52.0 1.8 fusion.73
  53.8 2.0 convolution_bitcast_fusion.7
  55.8 1.3 multiply_add_fusion.4
  57.0 1.2 fusion.74
  58.2 0.9 maximum_add_fusion.5
  59.1 1.7 maximum_add_fusion.4
  60.8 9.5 %dynamic_update_slice.6 = f32[3,512,512]{2,1,0:T(8,128)} dynamic-update-slice(f32[3,512,512]{2,1,0:T(8,128)} %get-tuple-element.303, f32[3,256,256]{2,1,0:T(8,128)S(1)} %maximum_add_fusion.4, s32[]{:T(128)} %constant.39.clone.1..sunk, s32[]{:T(128)S(6)} %select_n.64, s32[]{:T(128)S(6)} %select_n.65) | dynamic-update-slice | bytes 1572868 | tf_op jit(solution)/shard_map/while/body/eval_jaxpr/dynamic_update_slice | solution.py:112
  74.6 2.0 fusion.72
  76.6 1.9 convolution_bitcast_fusion.6
  78.5 1.8 fusion.73
  80.2 2.0 convolution_bitcast_fusion.7
  82.2 1.3 multiply_add_fusion.4
  83.5 1.2 fusion.74
  84.7 1.9 maximum_add_fusion.5
  86.6 1.7 maximum_add_fusion.4
  88.2 9.4 %dynamic_update_slice.6 = f32[3,512,512]{2,1,0:T(8,128)} dynamic-update-slice(f32[3,512,512]{2,1,0:T(8,128)} %get-tuple-element.303, f32[3,256,256]{2,1,0:T(8,128)S(1)} %maximum_add_fusion.4, s32[]{:T(128)} %constant.39.clone.1..sunk, s32[]{:T(128)S(6)} %select_n.64, s32[]{:T(128)S(6)} %select_n.65) | dynamic-update-slice | bytes 1572868 | tf_op jit(solution)/shard_map/while/body/eval_jaxpr/dynamic_update_slice | solution.py:112
  97.6 1.6 fusion.47
  99.3 3.0 %collective-permute-start.4 = (f32[3,128,512]{2,1,0:T(8,128)S(1)}, f32[3,128,512]{2,1,0:T(8,128)S(1)}, u32[]{:S(2)}, u32[]{:S(2)}) collective-permute-start(f32[3,128,512]{2,1,0:T(8,128)S(1)} %get-tuple-element.178), channel_id=1, source_target_pairs={{0,4},{4,8},{8,12},{1,5},{5,9},{9,13},{2,6},{6,10},{10,14},{3,7},{... | collective-permute-start | bytes 2359304 | tf_op jit(solution)/shard_map/ppermute | solution.py:13
  102.2 1.3 collective-permute-start.5
  103.5 14.3 %collective-permute-done.4 = f32[3,128,512]{2,1,0:T(8,128)S(1)} collective-permute-done((f32[3,128,512]{2,1,0:T(8,128)S(1)}, f32[3,128,512]{2,1,0:T(8,128)S(1)}, u32[]{:S(2)}, u32[]{:S(2)}) %collective-permute-start.4) | collective-permute-done | bytes 786464 | tf_op jit(solution)/shard_map/ppermute | solution.py:13
  117.8 4.2 %collective-permute-done.5 = f32[3,128,512]{2,1,0:T(8,128)S(1)} collective-permute-done((f32[3,128,512]{2,1,0:T(8,128)S(1)}, f32[3,128,512]{2,1,0:T(8,128)S(1)}, u32[]{:S(2)}, u32[]{:S(2)}) %collective-permute-start.5) | collective-permute-done | bytes 786464 | tf_op jit(solution)/shard_map/ppermute | solution.py:16
  122.3 0.9 fusion.48
  123.2 1.6 collective-permute-start.6
  124.9 1.3 collective-permute-start.7
  126.2 4.3 %collective-permute-done.6 = f32[3,256,128]{2,1,0:T(8,128)S(1)} collective-permute-done((f32[3,256,128]{2,1,0:T(8,128)}, f32[3,256,128]{2,1,0:T(8,128)S(1)}, u32[]{:S(2)}, u32[]{:S(2)}) %collective-permute-start.6) | collective-permute-done | bytes 393248 | tf_op jit(solution)/shard_map/ppermute | solution.py:13
  130.5 4.7 %collective-permute-done.7 = f32[3,256,128]{2,1,0:T(8,128)S(1)} collective-permute-done((f32[3,256,128]{2,1,0:T(8,128)}, f32[3,256,128]{2,1,0:T(8,128)S(1)}, u32[]{:S(2)}, u32[]{:S(2)}) %collective-permute-start.7) | collective-permute-done | bytes 393248 | tf_op jit(solution)/shard_map/ppermute | solution.py:16
  135.3 1.1 fusion.28
  136.4 81.3 %all-reduce.9.cloned.1.call-done = f32[2,256,256]{2,1,0:T(8,128)} async-done(((f32[2,256,256]{2,1,0:T(8,128)}), f32[2,256,256]{2,1,0:T(8,128)}) %all-reduce.9.cloned.1.call-update) | async-done | bytes 524304 | tf_op jit(solution)/shard_map/psum | solution.py:136
  217.6 1.9 multiply_add_fusion.1
  219.5 19.9 %all-reduce.7.cloned.1.call-done = f32[3,256,256]{2,1,0:T(8,128)} async-done(((f32[3,256,256]{2,1,0:T(8,128)}), f32[3,256,256]{2,1,0:T(8,128)}) %all-reduce.7.cloned.1.call-update) | async-done | bytes 786448 | tf_op jit(solution)/shard_map/psum | solution.py:132
  239.4 1.0 fusion.37
  240.4 1.9 fusion.29
  (32 shorter events, 5.0 us)
Async XLA Ops:
  7.2 13.6 %copy-start.3 = (f32[2,256,256]{2,1,0:T(8,128)S(1)}, f32[2,256,256]{2,1,0:T(8,128)}, u32[]{:S(2)}) copy-start(f32[2,256,256]{2,1,0:T(8,128)} %param.6) | copy-start | bytes 1572868
  7.2 210.5 %all-reduce.9.cloned.1.call-start = ((), (), s32[]{:S(2)}) async-start(), calls=%async_computation.1 | async-start | bytes 1048576 | tf_op jit(solution)/shard_map/psum | solution.py:136
  8.3 12.5 %collective-permute-start.1 = (f32[2,128,256]{2,1,0:T(8,128)S(1)}, f32[2,128,256]{2,1,0:T(8,128)S(1)}, u32[]{:S(2)}, u32[]{:S(2)}) collective-permute-start(f32[2,128,256]{2,1,0:T(8,128)S(1)} %get-tuple-element.186), channel_id=1, source_target_pairs={{4,0},{8,4},{12,8},{5,1},{9,5},{13,9},{6,2},{10,6},{14,10},{7,3},{... | collective-permute-start | bytes 786440 | tf_op jit(solution)/shard_map/ppermute | solution.py:16
  9.6 11.1 %collective-permute-start = (f32[2,128,256]{2,1,0:T(8,128)S(1)}, f32[2,128,256]{2,1,0:T(8,128)S(1)}, u32[]{:S(2)}, u32[]{:S(2)}) collective-permute-start(f32[2,128,256]{2,1,0:T(8,128)S(1)} %get-tuple-element.187), channel_id=1, source_target_pairs={{0,4},{4,8},{8,12},{1,5},{5,9},{9,13},{2,6},{6,10},{10,14},{3,7},{... | collective-permute-start | bytes 786440 | tf_op jit(solution)/shard_map/ppermute | solution.py:13
  20.9 7.4 %copy-start.1 = (f32[2,256,256]{2,1,0:T(8,128)S(1)}, f32[2,256,256]{2,1,0:T(8,128)}, u32[]{:S(2)}) copy-start(f32[2,256,256]{2,1,0:T(8,128)} %param.7) | copy-start | bytes 1572868
  21.8 13.9 %collective-permute-start.2 = (f32[2,512,128]{2,1,0:T(8,128)}, f32[2,512,128]{2,1,0:T(8,128)}, u32[]{:S(2)}, u32[]{:S(2)}) collective-permute-start(f32[2,512,128]{2,1,0:T(8,128)} %get-tuple-element.182), channel_id=1, source_target_pairs={{0,2},{1,3},{4,6},{5,7},{8,10},{9,11},{12,14},{13,15},{16,18},{17,... | collective-permute-start | bytes 1572872 | tf_op jit(solution)/shard_map/ppermute | solution.py:13
  26.1 14.2 %collective-permute-start.3 = (f32[2,512,128]{2,1,0:T(8,128)S(1)}, f32[2,512,128]{2,1,0:T(8,128)}, u32[]{:S(2)}, u32[]{:S(2)}) collective-permute-start(f32[2,512,128]{2,1,0:T(8,128)S(1)} %get-tuple-element.183), channel_id=1, source_target_pairs={{2,0},{3,1},{6,4},{7,5},{10,8},{11,9},{14,12},{15,13},{18,16},{19,... | collective-permute-start | bytes 1572872 | tf_op jit(solution)/shard_map/ppermute | solution.py:16
  41.8 2.0 copy-start.5
  97.6 24.3 %copy-start = (f32[3,512,512]{2,1,0:T(8,128)S(1)}, f32[3,512,512]{2,1,0:T(8,128)}, u32[]{:S(2)}) copy-start(f32[3,512,512]{2,1,0:T(8,128)} %get-tuple-element.93) | copy-start | bytes 9437188
  99.3 18.5 %collective-permute-start.4 = (f32[3,128,512]{2,1,0:T(8,128)S(1)}, f32[3,128,512]{2,1,0:T(8,128)S(1)}, u32[]{:S(2)}, u32[]{:S(2)}) collective-permute-start(f32[3,128,512]{2,1,0:T(8,128)S(1)} %get-tuple-element.178), channel_id=1, source_target_pairs={{0,4},{4,8},{8,12},{1,5},{5,9},{9,13},{2,6},{6,10},{10,14},{3,7},{... | collective-permute-start | bytes 2359304 | tf_op jit(solution)/shard_map/ppermute | solution.py:13
  102.2 19.7 %collective-permute-start.5 = (f32[3,128,512]{2,1,0:T(8,128)S(1)}, f32[3,128,512]{2,1,0:T(8,128)S(1)}, u32[]{:S(2)}, u32[]{:S(2)}) collective-permute-start(f32[3,128,512]{2,1,0:T(8,128)S(1)} %get-tuple-element.179), channel_id=1, source_target_pairs={{4,0},{8,4},{12,8},{5,1},{9,5},{13,9},{6,2},{10,6},{14,10},{7,3},{... | collective-permute-start | bytes 2359304 | tf_op jit(solution)/shard_map/ppermute | solution.py:16
  123.2 94.4 %copy-start.2 = (f32[2,256,256]{2,1,0:T(8,128)S(1)}, f32[2,256,256]{2,1,0:T(8,128)}, u32[]{:S(2)}) copy-start(f32[2,256,256]{2,1,0:T(8,128)} %param.7) | copy-start | bytes 1572868
  123.2 7.3 %collective-permute-start.6 = (f32[3,256,128]{2,1,0:T(8,128)}, f32[3,256,128]{2,1,0:T(8,128)S(1)}, u32[]{:S(2)}, u32[]{:S(2)}) collective-permute-start(f32[3,256,128]{2,1,0:T(8,128)} %get-tuple-element.180), channel_id=1, source_target_pairs={{0,2},{1,3},{4,6},{5,7},{8,10},{9,11},{12,14},{13,15},{16,18},{17,... | collective-permute-start | bytes 1179656 | tf_op jit(solution)/shard_map/ppermute | solution.py:13
  124.9 10.4 %collective-permute-start.7 = (f32[3,256,128]{2,1,0:T(8,128)}, f32[3,256,128]{2,1,0:T(8,128)S(1)}, u32[]{:S(2)}, u32[]{:S(2)}) collective-permute-start(f32[3,256,128]{2,1,0:T(8,128)} %get-tuple-element.181), channel_id=1, source_target_pairs={{2,0},{3,1},{6,4},{7,5},{10,8},{11,9},{14,12},{15,13},{18,16},{19,... | collective-permute-start | bytes 1179656 | tf_op jit(solution)/shard_map/ppermute | solution.py:16
  126.2 114.2 %copy-start.4 = (f32[2,256,256]{2,1,0:T(8,128)S(1)}, f32[2,256,256]{2,1,0:T(8,128)}, u32[]{:S(2)}) copy-start(f32[2,256,256]{2,1,0:T(8,128)} %param.6) | copy-start | bytes 1572868
  126.2 113.2 %all-reduce.7.cloned.1.call-start = ((), (), s32[]{:S(2)}) async-start(), calls=%async_computation | async-start | bytes 1572864 | tf_op jit(solution)/shard_map/psum | solution.py:132
Sparse Core Ops, SparseCore 0:
  126.3 91.2 all-reduce.8
  220.0 19.4 all-reduce.6
where the time goes:
time: 251 us; the launch traced here: 249 us
  waiting for transfers between devices  142 us (57%)
  other arithmetic  29.9 us (12%)
  local copies, waits for them, and re-layouts  28.3 us (11%)
  starting transfers between devices  19.8 us (8%)
  between operations  14.2 us (6%)
  matrix products  7.75 us (3%)
  loops' own time  7.59 us (3%)
    psum x1, waiting for transfers between devices, shards(): total_grad = lax.psum(probe_grad, ('scanx', 'scany', 'pos'))  81.3 us
    ppermute x4, waiting for transfers between devices, padded_2(): lax.ppermute(lax.slice_in_dim(block, block.shape[dim] - width, None, axis...  26.9 us
    psum x1, waiting for transfers between devices, shards(): core_sum = lax.psum(core_sum, 'pos')  19.9 us
    dynamic_update_slice x2, local copies, waits for them, and re-layouts, visit_position(): lax.dynamic_update_slice(object_grad, current + object_term, (zero_index,...  18.8 us
    ppermute x4, starting transfers between devices, padded_2(): lax.ppermute(lax.slice_in_dim(block, block.shape[dim] - width, None, axis...  14.5 us
    ppermute x4, waiting for transfers between devices, padded_2(): lax.ppermute(lax.slice_in_dim(block, 0, width, axis=dim), axis, backward)  13.6 us
    another operation x1, loops' own time, shards(): lax.scan(visit_position, (start_grad, start_probe), (amplitudes, offsets))  7.59 us
    ppermute x4, starting transfers between devices, padded_2(): lax.ppermute(lax.slice_in_dim(block, 0, width, axis=dim), axis, backward)  5.16 us
  transfers between devices with their start and end apart: 10, of which 9 were waited for; matrix products, arithmetic and copies ran while one was open for 3% of the time, Pallas kernels for 0%

commit v1 on v0

--- a/solution.py
+++ b/solution.py
@@ -133,7 +133,7 @@
     new_specimen = specimen + core_sum[0:2] / (core_sum[2:3] + 1.0)
     devices_count = lax.axis_size("scanx") * lax.axis_size("scany") * lax.axis_size("pos")
     step_size = 1.0 / math.sqrt(offsets.shape[0] * devices_count)
-    total_grad = lax.psum(probe_grad, ("scanx", "scany", "pos"))
+    total_grad = jnp.sum(lax.all_gather(probe_grad, ("scanx", "scany", "pos")), axis=0)
     new_probe = probe_wave + total_grad * step_size
     return (new_specimen, new_probe)
 

time: 251 us -> 225 us (0.90)
  waiting for transfers between devices: 142 us -> 113 us
  other arithmetic: 29.9 us -> 32.8 us
    psum x1 -> x0, waiting for transfers between devices: 81.3 us -> none  [shards(): total_grad = lax.psum(probe_grad, ('scanx', 'scany', 'pos'))]
    all_gather x0 -> x1, waiting for transfers between devices: none -> 55.3 us  [shards(): lax.all_gather(probe_grad, ('scanx', 'scany', 'pos'))]
    reduce_sum x0 -> x1, other arithmetic: none -> 4.03 us  [shards(): jnp.sum(lax.all_gather(probe_grad, ('scanx', 'scany', 'pos')), axis=0)]
    psum x1, waiting for transfers between devices: 19.9 us -> 17 us  [shards(): core_sum = lax.psum(core_sum, 'pos')]
  transfers between devices with their start and end apart: 10 -> 10, of which waited for: 9 -> 9; matrix products, arithmetic and copies ran while one was open for 3% -> 4% of each run, Pallas kernels for 0% -> 0%
where the time goes in v1:
time: 225 us; the launch traced here: 224 us
  waiting for transfers between devices  113 us (50%)
  other arithmetic  32.8 us (15%)
  local copies, waits for them, and re-layouts  27.4 us (12%)
  starting transfers between devices  19.8 us (9%)
  between operations  15.7 us (7%)
  matrix products  7.75 us (3%)
  loops' own time  7.59 us (3%)
    all_gather x1, waiting for transfers between devices, shards(): lax.all_gather(probe_grad, ('scanx', 'scany', 'pos'))  55.3 us
    ppermute x4, waiting for transfers between devices, padded_2(): lax.ppermute(lax.slice_in_dim(block, block.shape[dim] - width, None, axis...  26.5 us
    dynamic_update_slice x2, local copies, waits for them, and re-layouts, visit_position(): lax.dynamic_update_slice(object_grad, current + object_term, (zero_index,...  18.8 us
    psum x1, waiting for transfers between devices, shards(): core_sum = lax.psum(core_sum, 'pos')  17 us
    ppermute x4, starting transfers between devices, padded_2(): lax.ppermute(lax.slice_in_dim(block, block.shape[dim] - width, None, axis...  14.4 us
    ppermute x4, waiting for transfers between devices, padded_2(): lax.ppermute(lax.slice_in_dim(block, 0, width, axis=dim), axis, backward)  13.3 us
    another operation x1, loops' own time, shards(): lax.scan(visit_position, (start_grad, start_probe), (amplitudes, offsets))  7.59 us
    ppermute x4, starting transfers between devices, padded_2(): lax.ppermute(lax.slice_in_dim(block, 0, width, axis=dim), axis, backward)  5.29 us
  transfers between devices with their start and end apart: 10, of which 9 were waited for; matrix products, arithmetic and copies ran while one was open for 4% of the time, Pallas kernels for 0%

profile of v1, /device:TPU:0, one launch (start us, length us, event | category | flops | bytes accessed | tf_op | source)
XLA Modules:
  0.0 223.7 jit_solution(3575352932173154658)
XLA Ops:
  8.1 1.1 fusion.50
  9.2 1.3 collective-permute-start.1
  10.5 5.6 %collective-permute-start = (f32[2,128,256]{2,1,0:T(8,128)S(1)}, f32[2,128,256]{2,1,0:T(8,128)S(1)}, u32[]{:S(2)}, u32[]{:S(2)}) collective-permute-start(f32[2,128,256]{2,1,0:T(8,128)S(1)} %get-tuple-element.198), channel_id=1, source_target_pairs={{0,4},{4,8},{8,12},{1,5},{5,9},{9,13},{2,6},{6,10},{10,14},{3,7},{... | collective-permute-start | bytes 786440 | tf_op jit(solution)/shard_map/ppermute | solution.py:13
  16.1 1.0 fusion.41
  17.1 1.1 multiply_convert_fusion.1
  19.1 2.5 %collective-permute-done = f32[2,128,256]{2,1,0:T(8,128)S(1)} collective-permute-done((f32[2,128,256]{2,1,0:T(8,128)S(1)}, f32[2,128,256]{2,1,0:T(8,128)S(1)}, u32[]{:S(2)}, u32[]{:S(2)}) %collective-permute-start) | collective-permute-done | bytes 262176 | tf_op jit(solution)/shard_map/ppermute | solution.py:13
  21.7 0.9 fusion.49
  22.6 4.4 %collective-permute-start.2 = (f32[2,512,128]{2,1,0:T(8,128)}, f32[2,512,128]{2,1,0:T(8,128)}, u32[]{:S(2)}, u32[]{:S(2)}) collective-permute-start(f32[2,512,128]{2,1,0:T(8,128)} %get-tuple-element.193), channel_id=1, source_target_pairs={{0,2},{1,3},{4,6},{5,7},{8,10},{9,11},{12,14},{13,15},{16,18},{17,... | collective-permute-start | bytes 1572872 | tf_op jit(solution)/shard_map/ppermute | solution.py:13
  27.0 1.3 collective-permute-start.3
  30.6 5.9 %collective-permute-done.2 = f32[2,512,128]{2,1,0:T(8,128)} collective-permute-done((f32[2,512,128]{2,1,0:T(8,128)}, f32[2,512,128]{2,1,0:T(8,128)}, u32[]{:S(2)}, u32[]{:S(2)}) %collective-permute-start.2) | collective-permute-done | bytes 524320 | tf_op jit(solution)/shard_map/ppermute | solution.py:13
  36.5 4.7 %collective-permute-done.3 = f32[2,512,128]{2,1,0:T(8,128)} collective-permute-done((f32[2,512,128]{2,1,0:T(8,128)S(1)}, f32[2,512,128]{2,1,0:T(8,128)}, u32[]{:S(2)}, u32[]{:S(2)}) %collective-permute-start.3) | collective-permute-done | bytes 524320 | tf_op jit(solution)/shard_map/ppermute | solution.py:16
  41.2 1.4 pad_maximum_fusion
  42.6 2.0 broadcast_in_dim.10
  44.6 53.8 %while.14 = (s32[]{:T(128)}, f32[3,512,512]{2,1,0:T(8,128)}, f32[2,256,256]{2,1,0:T(8,128)}, s32[2,2]{1,0:T(2,128)S(1)}, f32[256,256]{1,0:T(8,128)}, /*index=5*/...) while((s32[]{:T(128)}, f32[3,512,512]{2,1,0:T(8,128)}, ...), condition=%wide.region_1.2_spmd.clone, body=%wide.region_0.1_spmd.clone.sunk | while | flops 540737536 | bytes 17170760 | solution.py:125
  49.0 2.0 fusion.72
  51.0 1.9 convolution_bitcast_fusion.6
  52.9 1.8 fusion.73
  54.6 2.0 convolution_bitcast_fusion.7
  56.6 1.3 multiply_add_fusion.4
  57.9 1.2 fusion.74
  59.1 0.9 maximum_add_fusion.5
  59.9 1.7 maximum_add_fusion.4
  61.6 9.5 %dynamic_update_slice.6 = f32[3,512,512]{2,1,0:T(8,128)} dynamic-update-slice(f32[3,512,512]{2,1,0:T(8,128)} %get-tuple-element.314, f32[3,256,256]{2,1,0:T(8,128)S(1)} %maximum_add_fusion.4, s32[]{:T(128)} %constant.40.clone.1..sunk, s32[]{:T(128)S(6)} %select_n.64, s32[]{:T(128)S(6)} %select_n.65) | dynamic-update-slice | bytes 1572868 | tf_op jit(solution)/shard_map/while/body/eval_jaxpr/dynamic_update_slice | solution.py:112
  75.4 2.0 fusion.72
  77.4 1.9 convolution_bitcast_fusion.6
  79.3 1.8 fusion.73
  81.1 2.0 convolution_bitcast_fusion.7
  83.0 1.3 multiply_add_fusion.4
  84.3 1.2 fusion.74
  85.5 1.9 maximum_add_fusion.5
  87.4 1.7 maximum_add_fusion.4
  89.1 9.4 %dynamic_update_slice.6 = f32[3,512,512]{2,1,0:T(8,128)} dynamic-update-slice(f32[3,512,512]{2,1,0:T(8,128)} %get-tuple-element.314, f32[3,256,256]{2,1,0:T(8,128)S(1)} %maximum_add_fusion.4, s32[]{:T(128)} %constant.40.clone.1..sunk, s32[]{:T(128)S(6)} %select_n.64, s32[]{:T(128)S(6)} %select_n.65) | dynamic-update-slice | bytes 1572868 | tf_op jit(solution)/shard_map/while/body/eval_jaxpr/dynamic_update_slice | solution.py:112
  98.4 1.6 fusion.47
  100.1 3.0 %collective-permute-start.4 = (f32[3,128,512]{2,1,0:T(8,128)S(1)}, f32[3,128,512]{2,1,0:T(8,128)S(1)}, u32[]{:S(2)}, u32[]{:S(2)}) collective-permute-start(f32[3,128,512]{2,1,0:T(8,128)S(1)} %get-tuple-element.189), channel_id=1, source_target_pairs={{0,4},{4,8},{8,12},{1,5},{5,9},{9,13},{2,6},{6,10},{10,14},{3,7},{... | collective-permute-start | bytes 2359304 | tf_op jit(solution)/shard_map/ppermute | solution.py:13
  103.0 1.3 collective-permute-start.5
  104.3 14.3 %collective-permute-done.4 = f32[3,128,512]{2,1,0:T(8,128)S(1)} collective-permute-done((f32[3,128,512]{2,1,0:T(8,128)S(1)}, f32[3,128,512]{2,1,0:T(8,128)S(1)}, u32[]{:S(2)}, u32[]{:S(2)}) %collective-permute-start.4) | collective-permute-done | bytes 786464 | tf_op jit(solution)/shard_map/ppermute | solution.py:13
  118.6 4.2 %collective-permute-done.5 = f32[3,128,512]{2,1,0:T(8,128)S(1)} collective-permute-done((f32[3,128,512]{2,1,0:T(8,128)S(1)}, f32[3,128,512]{2,1,0:T(8,128)S(1)}, u32[]{:S(2)}, u32[]{:S(2)}) %collective-permute-start.5) | collective-permute-done | bytes 786464 | tf_op jit(solution)/shard_map/ppermute | solution.py:16
  123.2 1.5 collective-permute-start.6
  124.7 1.4 collective-permute-start.7
  126.1 3.9 %collective-permute-done.6 = f32[3,256,128]{2,1,0:T(8,128)S(1)} collective-permute-done((f32[3,256,128]{2,1,0:T(8,128)S(1)}, f32[3,256,128]{2,1,0:T(8,128)S(1)}, u32[]{:S(2)}, u32[]{:S(2)}) %collective-permute-start.6) | collective-permute-done | bytes 393248 | tf_op jit(solution)/shard_map/ppermute | solution.py:13
  130.1 4.4 %collective-permute-done.7 = f32[3,256,128]{2,1,0:T(8,128)S(1)} collective-permute-done((f32[3,256,128]{2,1,0:T(8,128)S(1)}, f32[3,256,128]{2,1,0:T(8,128)S(1)}, u32[]{:S(2)}, u32[]{:S(2)}) %collective-permute-start.7) | collective-permute-done | bytes 393248 | tf_op jit(solution)/shard_map/ppermute | solution.py:16
  134.5 1.0 fusion.28
  136.2 17.0 %all-reduce.6.cloned.1.call-done = f32[3,256,256]{2,1,0:T(8,128)} async-done(((f32[3,256,256]{2,1,0:T(8,128)}), f32[3,256,256]{2,1,0:T(8,128)}) %all-reduce.6.cloned.1.call-update) | async-done | bytes 786448 | tf_op jit(solution)/shard_map/psum | solution.py:132
  153.2 1.0 fusion.37
  154.2 1.9 fusion.29
  156.1 55.3 %all-gather.3.cloned.1.call-done = f32[32,256,256]{2,1,0:T(8,128)} async-done(((f32[2,256,256]{2,1,0:T(8,128)}), f32[32,256,256]{2,1,0:T(8,128)}) %all-gather.3.cloned.1.call-update) | async-done | bytes 8388624 | tf_op jit(solution)/shard_map/all_gather | solution.py:136
  211.4 4.0 %reduce_sum.9 = f32[2,256,256]{2,1,0:T(8,128)S(1)} reduce(f32[16,2,256,256]{3,2,1,0:T(8,128)} %bitcast.152, f32[]{:T(128)} %constant.41.clone.1), dimensions={0}, to_apply=%region_3.4 | reduce | flops 1966080 | bytes 8912900 | tf_op jit(solution)/shard_map/reduce_sum | solution.py:136
  215.4 0.9 multiply_add_fusion.1
  (33 shorter events, 5.6 us)
Async XLA Ops:
  8.0 13.6 %copy-start.1 = (f32[2,256,256]{2,1,0:T(8,128)S(1)}, f32[2,256,256]{2,1,0:T(8,128)}, u32[]{:S(2)}) copy-start(f32[2,256,256]{2,1,0:T(8,128)} %param.6) | copy-start | bytes 1572868
  8.0 145.2 %all-reduce.6.cloned.1.call-start = ((), (), s32[]{:S(2)}) async-start(), calls=%async_computation | async-start | bytes 1572864 | tf_op jit(solution)/shard_map/psum | solution.py:132
  9.2 12.5 %collective-permute-start.1 = (f32[2,128,256]{2,1,0:T(8,128)S(1)}, f32[2,128,256]{2,1,0:T(8,128)S(1)}, u32[]{:S(2)}, u32[]{:S(2)}) collective-permute-start(f32[2,128,256]{2,1,0:T(8,128)S(1)} %get-tuple-element.197), channel_id=1, source_target_pairs={{4,0},{8,4},{12,8},{5,1},{9,5},{13,9},{6,2},{10,6},{14,10},{7,3},{... | collective-permute-start | bytes 786440 | tf_op jit(solution)/shard_map/ppermute | solution.py:16
  10.5 11.1 %collective-permute-start = (f32[2,128,256]{2,1,0:T(8,128)S(1)}, f32[2,128,256]{2,1,0:T(8,128)S(1)}, u32[]{:S(2)}, u32[]{:S(2)}) collective-permute-start(f32[2,128,256]{2,1,0:T(8,128)S(1)} %get-tuple-element.198), channel_id=1, source_target_pairs={{0,4},{4,8},{8,12},{1,5},{5,9},{9,13},{2,6},{6,10},{10,14},{3,7},{... | collective-permute-start | bytes 786440 | tf_op jit(solution)/shard_map/ppermute | solution.py:13
  21.7 7.4 %copy-start.3 = (f32[2,256,256]{2,1,0:T(8,128)S(1)}, f32[2,256,256]{2,1,0:T(8,128)}, u32[]{:S(2)}) copy-start(f32[2,256,256]{2,1,0:T(8,128)} %param.7) | copy-start | bytes 1572868
  22.6 13.9 %collective-permute-start.2 = (f32[2,512,128]{2,1,0:T(8,128)}, f32[2,512,128]{2,1,0:T(8,128)}, u32[]{:S(2)}, u32[]{:S(2)}) collective-permute-start(f32[2,512,128]{2,1,0:T(8,128)} %get-tuple-element.193), channel_id=1, source_target_pairs={{0,2},{1,3},{4,6},{5,7},{8,10},{9,11},{12,14},{13,15},{16,18},{17,... | collective-permute-start | bytes 1572872 | tf_op jit(solution)/shard_map/ppermute | solution.py:13
  27.0 14.2 %collective-permute-start.3 = (f32[2,512,128]{2,1,0:T(8,128)S(1)}, f32[2,512,128]{2,1,0:T(8,128)}, u32[]{:S(2)}, u32[]{:S(2)}) collective-permute-start(f32[2,512,128]{2,1,0:T(8,128)S(1)} %get-tuple-element.194), channel_id=1, source_target_pairs={{2,0},{3,1},{6,4},{7,5},{10,8},{11,9},{14,12},{15,13},{18,16},{19,... | collective-permute-start | bytes 1572872 | tf_op jit(solution)/shard_map/ppermute | solution.py:16
  42.6 2.0 copy-start.5
  98.4 24.3 %copy-start = (f32[3,512,512]{2,1,0:T(8,128)S(1)}, f32[3,512,512]{2,1,0:T(8,128)}, u32[]{:S(2)}) copy-start(f32[3,512,512]{2,1,0:T(8,128)} %get-tuple-element.93) | copy-start | bytes 9437188
  100.1 18.5 %collective-permute-start.4 = (f32[3,128,512]{2,1,0:T(8,128)S(1)}, f32[3,128,512]{2,1,0:T(8,128)S(1)}, u32[]{:S(2)}, u32[]{:S(2)}) collective-permute-start(f32[3,128,512]{2,1,0:T(8,128)S(1)} %get-tuple-element.189), channel_id=1, source_target_pairs={{0,4},{4,8},{8,12},{1,5},{5,9},{9,13},{2,6},{6,10},{10,14},{3,7},{... | collective-permute-start | bytes 2359304 | tf_op jit(solution)/shard_map/ppermute | solution.py:13
  103.0 19.7 %collective-permute-start.5 = (f32[3,128,512]{2,1,0:T(8,128)S(1)}, f32[3,128,512]{2,1,0:T(8,128)S(1)}, u32[]{:S(2)}, u32[]{:S(2)}) collective-permute-start(f32[3,128,512]{2,1,0:T(8,128)S(1)} %get-tuple-element.190), channel_id=1, source_target_pairs={{4,0},{8,4},{12,8},{5,1},{9,5},{13,9},{6,2},{10,6},{14,10},{7,3},{... | collective-permute-start | bytes 2359304 | tf_op jit(solution)/shard_map/ppermute | solution.py:16
  123.2 6.9 %collective-permute-start.6 = (f32[3,256,128]{2,1,0:T(8,128)S(1)}, f32[3,256,128]{2,1,0:T(8,128)S(1)}, u32[]{:S(2)}, u32[]{:S(2)}) collective-permute-start(f32[3,256,128]{2,1,0:T(8,128)S(1)} %get-tuple-element.191), channel_id=1, source_target_pairs={{0,2},{1,3},{4,6},{5,7},{8,10},{9,11},{12,14},{13,15},{16,18},{17,... | collective-permute-start | bytes 1179656 | tf_op jit(solution)/shard_map/ppermute | solution.py:13
  124.7 29.5 %copy-start.2 = (f32[2,256,256]{2,1,0:T(8,128)S(1)}, f32[2,256,256]{2,1,0:T(8,128)}, u32[]{:S(2)}) copy-start(f32[2,256,256]{2,1,0:T(8,128)} %param.6) | copy-start | bytes 1572868
  124.7 9.8 %collective-permute-start.7 = (f32[3,256,128]{2,1,0:T(8,128)S(1)}, f32[3,256,128]{2,1,0:T(8,128)S(1)}, u32[]{:S(2)}, u32[]{:S(2)}) collective-permute-start(f32[3,256,128]{2,1,0:T(8,128)S(1)} %get-tuple-element.192), channel_id=1, source_target_pairs={{2,0},{3,1},{6,4},{7,5},{10,8},{11,9},{14,12},{15,13},{18,16},{19,... | collective-permute-start | bytes 1179656 | tf_op jit(solution)/shard_map/ppermute | solution.py:16
  135.6 75.8 %all-gather.3.cloned.1.call-start = ((), (), s32[]{:S(2)}) async-start(), calls=%async_computation.1 | async-start | bytes 8912896 | tf_op jit(solution)/shard_map/all_gather | solution.py:136
  211.4 4.0 %copy-start.4 = (f32[2,256,256]{2,1,0:T(8,128)S(1)}, f32[2,256,256]{2,1,0:T(8,128)}, u32[]{:S(2)}) copy-start(f32[2,256,256]{2,1,0:T(8,128)} %param.7) | copy-start | bytes 1572868
Sparse Core Ops, SparseCore 0:
  135.7 17.4 all-reduce.5
Sparse Core Ops, SparseCore 1:
  138.8 72.5 all-gather.2
